TPU v7x, 32 devices: a whole 2x2x4 slice. The times are simulated.
32 devices in a mesh: section: 2 (over y), expert: 16 (over z, x, core).
Axes of the slice: x: 2, y: 2, z: 4, core: 2. Of those that a mesh axis runs over, the one named last changes fastest.
Arguments:
- tokens: bfloat16 [2048, 7168], P('expert', 'section'), may hold values from -6 to 6
- exponents: int32 [2048, 56], P('expert', 'section'), may hold values from -9 to -5
- expert_ids: int32 [2048, 8], P('expert'), may hold values from 0 to 15, all different within a row; in each aligned block of 128 rows (0 to 127, 128 to 255, ...) at most 80 rows name the same one
- affinity: float32 [2048, 8], P('expert'), may hold values from 0.1 to 1
- w_gate: bfloat16 [16, 7168, 2048], P('expert', None, 'section'), may hold values from -0.0625 to 0.0625
- w_up: bfloat16 [16, 7168, 2048], P('expert', None, 'section'), may hold values from -0.0625 to 0.0625
- w_down: bfloat16 [16, 2048, 7168], P('expert', 'section'), may hold values from -0.125 to 0.125
Outputs:
- moe_out: bfloat16 [2048, 7168], P('expert', 'section')
Inputs may be any that keep to these rules, and one draw needn't show every extreme that they name: `expert_ids`: each row names 8 different experts. In the 128 rows of one token group no expert is named more than 80 times, a bound that some block reaches.
All inputs are finite; a program needn't handle non-finite values.
Results may differ from a plain program's by a relative error of at most 0.012.
Values may be sent and summed in bfloat16 or wider, within the bound.
No kernel may reach another device: no remote copies, remote signals or barrier semaphores. Data moves between devices by JAX's collectives and lax.ppermute only.
A program may use at most 192 MiB of HBM per device.

v0:
```python
import jax
import jax.numpy as jnp
from jax import lax
from jax.sharding import PartitionSpec as P

quant_limit = 448.0
route_scaling = 2.5


def slot_positions(ids, capacity, experts):
    flat = ids.reshape(-1)
    marks = (flat[:, None] == jnp.arange(experts, dtype=jnp.int32)[None, :]).astype(jnp.int32)
    before = jnp.cumsum(marks, axis=0) - marks
    slot = jnp.sum(before * marks, axis=1)
    return (flat * capacity + slot).reshape(ids.shape)


def body(tokens, exponents, expert_ids, affinity, w_gate, w_up, w_down):
    tok_rows, width = tokens.shape
    tile_count = width // 128
    top_count = expert_ids.shape[1]
    section_count = lax.axis_size("section")
    expert_count = lax.axis_size("expert")
    capacity = min(tok_rows, tok_rows * top_count * 5 // (4 * expert_count))
    slot_total = expert_count * capacity
    scales = jnp.exp2(exponents.astype(jnp.float32))
    tiles = tokens.astype(jnp.float32).reshape(tok_rows, tile_count, 128) / scales[:, :, None]
    quant = jnp.clip(tiles, -quant_limit, quant_limit).astype(jnp.bfloat16).reshape(tok_rows, width)
    slot_index = slot_positions(expert_ids, capacity, expert_count)
    columns = jnp.arange(slot_total, dtype=jnp.int32)
    select = jnp.any(slot_index[:, :, None] == columns[None, None, :], axis=1)
    contract = (((0,), (0,)), ((), ()))
    send_tiles = lax.dot_general(
        select.astype(jnp.bfloat16), quant, contract, preferred_element_type=jnp.float32
    ).astype(jnp.bfloat16)
    send_scales = lax.dot_general(
        select.astype(jnp.float32), scales, contract, precision=lax.Precision.HIGHEST
    ).astype(jnp.bfloat16)
    got_tiles, got_scales = (
        lax.all_to_all(
            send_tiles.reshape(expert_count, capacity, width),
            "expert",
            split_axis=0,
            concat_axis=0,
            tiled=True,
        ),
        lax.all_to_all(
            send_scales.reshape(expert_count, capacity, tile_count),
            "expert",
            split_axis=0,
            concat_axis=0,
            tiled=True,
        ),
    )
    all_tiles, all_scales = (
        lax.all_gather(got_tiles[None], "section", axis=0, tiled=True),
        lax.all_gather(got_scales[None], "section", axis=0, tiled=True),
    )
    restored = (
        all_tiles.reshape(section_count, expert_count, capacity, tile_count, 128)
        * all_scales[..., None]
    ).reshape(section_count, slot_total, width)
    hidden_local = w_gate.shape[2]
    gate = jnp.einsum(
        "srd,sdf->rf",
        restored,
        w_gate[0].reshape(section_count, width, hidden_local),
        preferred_element_type=jnp.float32,
    )
    up = jnp.einsum(
        "srd,sdf->rf",
        restored,
        w_up[0].reshape(section_count, width, hidden_local),
        preferred_element_type=jnp.float32,
    )
    hidden = (jax.nn.silu(gate) * up).astype(jnp.bfloat16)
    partial_rows = jnp.einsum(
        "rf,fsd->srd",
        hidden,
        w_down[0].reshape(hidden_local, section_count, width),
        preferred_element_type=jnp.float32,
    ).astype(jnp.bfloat16)
    summed = lax.psum_scatter(partial_rows, "section", scatter_dimension=0, tiled=True).astype(
        jnp.float32
    )
    summed_rows = summed.astype(jnp.bfloat16).reshape(expert_count, capacity, width)
    expert_rows = lax.all_to_all(summed_rows, "expert", split_axis=0, concat_axis=0, tiled=True)
    flat_rows = expert_rows.reshape(slot_total, width)
    picked = jnp.take(flat_rows, slot_index, axis=0)
    route_weight = route_scaling * affinity / jnp.sum(affinity, axis=1, keepdims=True)
    total = jnp.sum(picked.astype(jnp.float32) * route_weight[:, :, None], axis=1)
    return total.astype(jnp.bfloat16)


def solution(mesh):
    return jax.shard_map(
        body,
        mesh=mesh,
        in_specs=(
            P("expert", "section"),
            P("expert", "section"),
            P("expert", None),
            P("expert", None),
            P("expert", None, "section"),
            P("expert", None, "section"),
            P("expert", "section", None),
        ),
        out_specs=P("expert", "section"),
        check_vma=False,
    )
```

profile of v0, /device:TPU:11, one launch (start us, length us, event | category | flops | bytes accessed | tf_op | source)
XLA Modules:
  0.0 986.0 jit_solution(10012667298380749259)
XLA Ops:
  6.5 0.0 all-gather.4.cloned.1.call-start
  6.5 0.8 copy.61
  7.3 0.1 eq.42
  7.4 0.1 eq.38
  7.5 4.5 reduce-window.6
  12.0 0.1 slice.10
  12.1 0.1 copy.63
  12.3 0.1 copy.64
  12.4 0.1 broadcast_add_fusion
  12.5 0.1 reduce_sum.30
  12.6 1.3 compare_and_fusion
  13.9 0.1 copy.67
  14.0 0.5 copy-done
  14.5 1.6 fusion.6
  16.2 1.6 copy.68
  17.7 0.7 multiply_exponential_fusion
  18.4 0.2 fusion.9
  18.7 2.6 convolution_convert_fusion.1
  21.3 205.4 %all_to_all.15 = bf16[16,80,3584]{2,1,0:T(8,128)(2,1)} all-to-all(bf16[16,80,3584]{2,1,0:T(8,128)(2,1)S(1)} %bitcast.71), channel_id=1, replica_groups=mesh['section'=2,'expert'=16] {'expert'}, dimensions={0} | all-to-all | bytes 18350080 | tf_op jit(solution)/shard_map/all_to_all | solution.py:40
  226.7 0.0 all-gather.4.cloned.1.call-update
  226.7 0.7 copy-done.3
  227.4 0.3 convolution_convert_fusion.2
  227.7 0.2 reshape.59
  227.9 0.7 copy.69
  228.6 5.7 all-to-all-start.1
  234.2 0.0 reduce-scatter.2.cloned.1.call-start
  234.3 33.0 %reshape_squeeze.11 = bf16[1024,2,3584]{2,1,0:T(2,128)(2,1)} reshape(bf16[1,1024,7168]{2,1,0:T(8,128)(2,1)} %param.13) | data formatting | bytes 29360128 | tf_op jit(solution)/shard_map/reshape;squeeze | solution.py:80
  267.2 0.0 all-to-all-done.1
  267.3 8.5 all-gather.1
  275.8 0.4 copy.71
  276.2 13.6 %mul.47 = bf16[2,16,80,28,128]{4,3,2,1,0:T(8,128)(2,1)} broadcast(bf16[2,16,80,28]{3,2,1,0:T(8,128)(2,1)S(1)} %copy.71), dimensions={0,1,2,3} | broadcast | bytes 18493440 | tf_op jit(solution)/shard_map/mul | solution.py:60
  289.8 29.7 %mul.48 = bf16[2,1280,3584]{2,1,0:T(8,128)(2,1)} reshape(bf16[2,16,80,28,128]{4,3,2,1,0:T(8,128)(2,1)} %mul.47) | data formatting | bytes 36700160 | tf_op jit(solution)/shard_map/mul | solution.py:60
  319.5 128.6 %all-gather.4.cloned.1.call-done = bf16[32,80,3584]{2,1,0:T(8,128)(2,1)} async-done(((bf16[16,80,3584]{2,1,0:T(8,128)(2,1)}), bf16[32,80,3584]{2,1,0:T(8,128)(2,1)}) %all-gather.4.cloned.1.call-update) | async-done | bytes 18350096 | tf_op jit(solution)/shard_map/all_gather | solution.py:56
  448.1 12.9 %bitcast_multiply_fusion = bf16[2,1280,3584]{2,1,0:T(8,128)(2,1)S(1)} fusion(bf16[2,1280,3584]{2,1,0:T(8,128)(2,1)} %mul.48, bf16[2,1280,3584]{2,1,0:T(8,128)(2,1)} %bitcast.72), kind=kLoop, calls=%fused_computation.2 | loop fusion | flops 9175040 | bytes 55050240 | tf_op jit(solution)/shard_map/mul | solution.py:60
  461.0 23.7 %fusion.15 = f32[1280,1024,1]{1,0,2:T(8,128)} fusion(bf16[2,1280,3584]{2,1,0:T(8,128)(2,1)S(1)} %bitcast_multiply_fusion, bf16[2,3584,1024]{2,1,0:T(8,128)(2,1)} %bitcast.77), kind=kOutput, calls=%fused_computation.37 | convolution fusion | flops 18790481920 | bytes 38273024 | tf_op jit(solution)/shard_map/srd,sdf->rf/dot_general | solution.py:70
  484.7 23.6 %fusion.7 = bf16[1280,1024,1]{1,0,2:T(8,128)(2,1)S(1)} fusion(f32[1280,1024,1]{1,0,2:T(8,128)} %fusion.15, bf16[2,1280,3584]{2,1,0:T(8,128)(2,1)S(1)} %bitcast_multiply_fusion, bf16[2,3584,1024]{2,1,0:T(8,128)(2,1)} %bitcast.78), kind=kOutput, calls=%fused_computation.17 | convolution fusion | flops 18798346240 | bytes 40894464 | tf_op jit(solution)/shard_map/srd,sdf->rf/dot_general | solution.py:64
  508.2 26.9 %fusion = bf16[2,1280,3584]{2,1,0:T(8,128)(2,1)} fusion(bf16[1280,1024,1]{1,0,2:T(8,128)(2,1)S(1)} %fusion.7, bf16[1024,2,3584]{2,1,0:T(2,128)(2,1)} %reshape_squeeze.11), kind=kOutput, calls=%fused_computation.3 | convolution fusion | flops 18799656960 | bytes 35651584 | tf_op jit(solution)/shard_map/rf,fsd->srd/dot_general | solution.py:77
  535.1 0.0 reduce-scatter.2.cloned.1.call-update
  535.1 206.3 %reduce-scatter.2.cloned.1.call-done = bf16[1,1280,3584]{2,1,0:T(8,128)(2,1)} async-done(((bf16[2,1280,3584]{2,1,0:T(8,128)(2,1)}), bf16[1,1280,3584]{2,1,0:T(8,128)(2,1)}) %reduce-scatter.2.cloned.1.call-update) | async-done | bytes 9175056 | tf_op jit(solution)/shard_map/reduce_scatter | solution.py:83
  741.4 6.6 all-to-all-start.2
  748.0 0.0 copy-done.1
  748.0 0.1 copy.73
  748.1 0.1 reshape.64
  748.3 0.1 copy.66
  748.4 0.1 copy.74
  748.5 198.7 %all-to-all-done.2 = bf16[16,80,3584]{2,1,0:T(8,128)(2,1)} async-done(((bf16[16,80,3584]{2,1,0:T(8,128)(2,1)}), bf16[16,80,3584]{2,1,0:T(8,128)(2,1)}, u32[]{:S(2)}, u32[]{:S(2)}) %all-to-all-start.2) | async-done | bytes 9175072 | tf_op jit(solution)/shard_map/all_to_all | solution.py:87
  947.2 18.6 %gather_fusion = bf16[1024,3584]{1,0:T(8,128)(2,1)} fusion(bf16[1280,3584]{1,0:T(8,128)(2,1)} %bitcast.13, s32[1024]{0:T(1024)S(1)} %broadcast_clamp_fusion), kind=kCustom, calls=%fused_computation | custom fusion | bytes 14684160 | tf_op jit(solution)/shard_map/jit(_take)/gather | solution.py:89
  965.8 13.3 %multiply_reduce_fusion = bf16[128,3584]{1,0:T(8,128)(2,1)} fusion(bf16[1024,3584]{1,0:T(8,128)(2,1)} %gather_fusion, f32[128,8]{1,0:T(8,128)S(1)} %copy.74, pred[128,8]{1,0:T(8,128)(4,1)S(1)} %copy.66), kind=kLoop, calls=%fused_computation.6 | loop fusion | flops 14221312 | bytes 8262656 | tf_op jit(solution)/shard_map/reduce_sum | solution.py:91
  (17 shorter events, 0.2 us)
Async XLA Ops:
  6.5 441.5 %all-gather.4.cloned.1.call-start = ((), (), s32[]{:S(2)}) async-start(), calls=%async_computation.5 | async-start | bytes 27525120 | tf_op jit(solution)/shard_map/all_gather | solution.py:56
  13.9 0.6 copy-start
  226.7 0.7 copy-start.3
  228.6 38.7 %all-to-all-start.1 = ((bf16[16,80,28]{1,2,0:T(8,128)(2,1)}), bf16[16,80,28]{1,2,0:T(8,128)(2,1)S(1)}, u32[]{:S(2)}, u32[]{:S(2)}) async-start(bf16[16,80,28]{1,2,0:T(8,128)(2,1)} %copy.69), calls=%async_computation.1 | async-start | bytes 262144 | tf_op jit(solution)/shard_map/all_to_all | solution.py:47
  234.2 507.2 %reduce-scatter.2.cloned.1.call-start = ((), (), s32[]{:S(2)}) async-start(), calls=%async_computation.4 | async-start | bytes 27525120 | tf_op jit(solution)/shard_map/reduce_scatter | solution.py:83
  741.4 6.6 copy-start.1
  741.4 6.9 copy-start.4
  741.4 7.0 copy-start.2
  741.4 205.8 %all-to-all-start.2 = ((bf16[16,80,3584]{2,1,0:T(8,128)(2,1)}), bf16[16,80,3584]{2,1,0:T(8,128)(2,1)}, u32[]{:S(2)}, u32[]{:S(2)}) async-start(bf16[16,80,3584]{2,1,0:T(8,128)(2,1)} %bitcast.73), calls=%async_computation.3 | async-start | bytes 18350080 | tf_op jit(solution)/shard_map/all_to_all | solution.py:87
Sparse Core Ops, SparseCore 0:
  226.8 221.2 all-gather.3
  535.2 206.0 reduce-scatter.1
where the time goes:
time: 988 us; the launch traced here: 986 us
  waiting for transfers between devices  534 us (54%)
  blocking collectives  214 us (22%)
  local copies, waits for them, and re-layouts  101 us (10%)
  matrix products  77 us (8%)
  other arithmetic  34.8 us (4%)
  between operations  13.5 us (1%)
  starting transfers between devices  12.4 us (1%)
    reduce_scatter x1, waiting for transfers between devices, body(): lax.psum_scatter(partial_rows, 'section', scatter_dimension=0, tiled=True)  206 us
    all_to_all x1, blocking collectives, body(): lax.all_to_all(send_tiles.reshape(expert_count, capacity, width), 'expert...  205 us
    all_to_all x1, waiting for transfers between devices, body(): lax.all_to_all(summed_rows, 'expert', split_axis=0, concat_axis=0, tiled=...  199 us
    all_gather x1, waiting for transfers between devices, body(): lax.all_gather(got_tiles[None], 'section', axis=0, tiled=True)  129 us
    mul x2, local copies, waits for them, and re-layouts, body(): all_tiles.reshape(section_count, expert_count, capacity, tile_count, 128)  43.3 us
    another operation x1, local copies, waits for them, and re-layouts, body(): w_down[0].reshape(hidden_local, section_count, width)  33 us
    dot_general x1, matrix products, body(): jnp.einsum('rf,fsd->srd', hidden, w_down[0].reshape(hidden_local, section...  26.9 us
    dot_general x1, matrix products, body(): jnp.einsum('srd,sdf->rf', restored, w_up[0].reshape(section_count, width,...  23.7 us
  transfers between devices with their start and end apart: 4, of which 3 were waited for; matrix products, arithmetic and copies ran while one was open for 8% of the time, Pallas kernels for 0%

commit v1 on v0

--- a/solution.py
+++ b/solution.py
@@ -1,10 +1,169 @@
+import functools
+
 import jax
 import jax.numpy as jnp
 from jax import lax
+from jax.experimental import pallas as pl
+from jax.experimental.pallas import tpu as pltpu
 from jax.sharding import PartitionSpec as P
+
 
 quant_limit = 448.0
 route_scaling = 2.5
+lane = 128
+
+
+def restore_kernel(scales_ref, tokens_ref, out_ref):
+    for tile in range(tokens_ref.shape[1] // lane):
+        span = slice(tile * lane, (tile + 1) * lane)
+        scale = scales_ref[:, tile : tile + 1]
+        quant = jnp.clip(tokens_ref[:, span].astype(jnp.float32) / scale, -quant_limit, quant_limit)
+        restored = quant.astype(jnp.bfloat16).astype(jnp.float32) * scale
+        out_ref[:, span] = restored.astype(jnp.bfloat16)
+
+
+def restore(tokens, scales):
+    return pl.pallas_call(
+        restore_kernel,
+        out_shape=jax.ShapeDtypeStruct(tokens.shape, jnp.bfloat16),
+        cost_estimate=pl.CostEstimate(
+            flops=4 * tokens.size, bytes_accessed=4 * tokens.size, transcendentals=0
+        ),
+        name="restore",
+    )(scales, tokens)
+
+
+def up_kernel(units, cap, side_ref, pick_ref, weight_ref, *refs):
+    mine, theirs = refs[:units], refs[units : 2 * units]
+    gate_ref, up_ref, hidden_ref, rows_ref, gate_sum, up_sum = refs[2 * units :]
+    step = pl.program_id(0)
+    part = pl.program_id(1)
+    side = side_ref[0]
+
+    @pl.when((step == 0) & (part == 0))
+    def _():
+        for unit in range(units):
+            span = slice(unit * cap, (unit + 1) * cap)
+            for source, place in ((mine[unit], side), (theirs[unit], 1 - side)):
+                rows_ref[place, span, :] = jnp.dot(
+                    pick_ref[unit], source[...], preferred_element_type=jnp.float32
+                ).astype(jnp.bfloat16)
+
+    @pl.when(part == 0)
+    def _():
+        gate_sum[...] = jnp.zeros_like(gate_sum)
+        up_sum[...] = jnp.zeros_like(up_sum)
+
+    rows = rows_ref[part]
+    gate_sum[...] += jnp.dot(rows, gate_ref[...], preferred_element_type=jnp.float32)
+    up_sum[...] += jnp.dot(rows, up_ref[...], preferred_element_type=jnp.float32)
+
+    @pl.when(part == 1)
+    def _():
+        gate = gate_sum[...]
+        hidden = gate / (1.0 + jnp.exp(-gate)) * up_sum[...] * weight_ref[...]
+        hidden_ref[...] = hidden.astype(jnp.bfloat16)
+
+
+def down_kernel(units, cap, half_steps, side_ref, put_ref, hidden_ref, down_ref, *refs):
+    outs, rows_ref = refs[: 2 * units], refs[2 * units]
+    step = pl.program_id(0)
+    rows_ref[...] = jnp.dot(
+        hidden_ref[...], down_ref[...], preferred_element_type=jnp.float32
+    ).astype(jnp.bfloat16)
+
+    def finish(targets):
+        for unit in range(units):
+            targets[unit][...] = jnp.dot(
+                put_ref[unit],
+                rows_ref[unit * cap : (unit + 1) * cap, :],
+                preferred_element_type=jnp.float32,
+            ).astype(jnp.bfloat16)
+
+    @pl.when(step < half_steps)
+    def _():
+        finish(outs[:units])
+
+    @pl.when(step >= half_steps)
+    def _():
+        finish(outs[units:])
+
+
+def single(shape):
+    return pl.BlockSpec(shape, lambda *_: (0,) * len(shape), pipeline_mode=pl.Buffered(1))
+
+
+def quarter_of(quarter, shape):
+    place = (quarter,) + (0,) * (len(shape) - 1)
+    return pl.BlockSpec(shape, lambda *_: place, pipeline_mode=pl.Buffered(1))
+
+
+def ffn_up(quarter, side, pick, weight, mine, theirs, w_gate, w_up):
+    units = len(mine)
+    tokens, width = mine[0].shape
+    cap = pick.shape[1]
+    hidden = w_gate.shape[1]
+    wide = 512 if hidden % 512 == 0 else hidden
+    rows = units * cap
+    tile = pl.BlockSpec((width, wide), lambda n, k, s: (k, n))
+    return pl.pallas_call(
+        functools.partial(up_kernel, units, cap),
+        out_shape=jax.ShapeDtypeStruct((rows, hidden), jnp.bfloat16),
+        grid_spec=pltpu.PrefetchScalarGridSpec(
+            num_scalar_prefetch=1,
+            grid=(hidden // wide, 2),
+            in_specs=[quarter_of(quarter, (units, cap, tokens)), quarter_of(quarter, (rows, 1))]
+            + [single((tokens, width))] * (2 * units)
+            + [tile, tile],
+            out_specs=pl.BlockSpec((rows, wide), lambda n, k, s: (0, n)),
+            scratch_shapes=[
+                pltpu.VMEM((2, rows, width), jnp.bfloat16),
+                pltpu.VMEM((rows, wide), jnp.float32),
+                pltpu.VMEM((rows, wide), jnp.float32),
+            ],
+        ),
+        compiler_params=pltpu.CompilerParams(dimension_semantics=("arbitrary", "arbitrary")),
+        cost_estimate=pl.CostEstimate(
+            flops=8 * rows * hidden * width,
+            bytes_accessed=8 * hidden * width + 4 * units * tokens * width,
+            transcendentals=rows * hidden,
+        ),
+        name="ffn_up",
+    )(side, pick, weight, *mine, *theirs, w_gate, w_up)
+
+
+def ffn_down(quarter, side, put, hidden_rows, w_down, width):
+    _, tokens, cap = put.shape
+    rows, hidden = hidden_rows.shape
+    units = rows // cap
+    half_steps = 2
+    tall = width // half_steps
+
+    def down_map(j, s):
+        far = j >= half_steps
+        return (0, jnp.where(far, (1 - s[0]) * half_steps + j - half_steps, s[0] * half_steps + j))
+
+    out = jax.ShapeDtypeStruct((tokens, width), jnp.bfloat16)
+    results = pl.pallas_call(
+        functools.partial(down_kernel, units, cap, half_steps),
+        out_shape=[out] * (2 * units),
+        grid_spec=pltpu.PrefetchScalarGridSpec(
+            num_scalar_prefetch=1,
+            grid=(2 * half_steps,),
+            in_specs=[quarter_of(quarter, (units, tokens, cap)), single(hidden_rows.shape), pl.BlockSpec((hidden, tall), down_map)],
+            out_specs=[pl.BlockSpec((tokens, tall), lambda j, s: (0, jnp.minimum(j, half_steps - 1)))] * units
+            + [pl.BlockSpec((tokens, tall), lambda j, s: (0, jnp.maximum(j - half_steps, 0)))] * units,
+            scratch_shapes=[pltpu.VMEM((rows, tall), jnp.bfloat16)],
+        ),
+        compiler_params=pltpu.CompilerParams(dimension_semantics=("arbitrary",)),
+        cost_estimate=pl.CostEstimate(
+            flops=4 * rows * hidden * width,
+            bytes_accessed=4 * hidden * width + 4 * units * tokens * width,
+            transcendentals=0,
+        ),
+        name="ffn_down",
+    )(side, put, hidden_rows, w_down)
+    return results[:units], results[units:]
 
 
 def slot_positions(ids, capacity, experts):
@@ -15,7 +174,7 @@
     return (flat * capacity + slot).reshape(ids.shape)
 
 
-def body(tokens, exponents, expert_ids, affinity, w_gate, w_up, w_down):
+def exchange_body(tokens, exponents, expert_ids, affinity, w_gate, w_up, w_down):
     tok_rows, width = tokens.shape
     tile_count = width // 128
     top_count = expert_ids.shape[1]
@@ -92,7 +251,164 @@
     return total.astype(jnp.bfloat16)
 
 
+def pairs(size, flip):
+    return [(index, index ^ flip) for index in range(size)]
+
+
+def joined(*terms):
+    total = terms[0].astype(jnp.float32)
+    for term in terms[1:]:
+        total += term.astype(jnp.float32)
+    return total.astype(jnp.bfloat16)
+
+
+def after(value, *deps):
+    return lax.optimization_barrier((value, *deps))[0] if deps else value
+
+
+def routing_table(expert_ids, affinity, experts):
+    weight = route_scaling * affinity / jnp.sum(affinity, axis=1, keepdims=True)
+    chosen = expert_ids[:, :, None] == jnp.arange(experts, dtype=jnp.int32)[None, None, :]
+    table = jnp.sum(jnp.where(chosen, weight[:, :, None], 0.0), axis=1).T
+    return lax.all_to_all(table, "expert", split_axis=0, concat_axis=0, tiled=True)
+
+
+def routing_slots(table, places, capacity):
+    me = lax.axis_index("expert")
+    table = jnp.take(table, me ^ jnp.array(places, jnp.int32), axis=0)
+    named = table > 0
+    count = table.shape[1]
+    ordered = jnp.arange(count)[:, None] <= jnp.arange(count)[None, :]
+    slot = jnp.dot(
+        named.astype(jnp.bfloat16), ordered.astype(jnp.bfloat16), preferred_element_type=jnp.float32
+    ).astype(jnp.int32) - 1
+    slot = jnp.where(named, slot, -1)
+    hits = slot[:, None, :] == jnp.arange(capacity, dtype=jnp.int32)[None, :, None]
+    slot_weight = jnp.sum(jnp.where(hits, table[:, None, :], 0.0), axis=2)
+    put = slot[:, :, None] == jnp.arange(capacity, dtype=jnp.int32)[None, None, :]
+    return hits.astype(jnp.bfloat16), put.astype(jnp.bfloat16), slot_weight.reshape(-1, 1)
+
+
+def grid_body(tokens, exponents, expert_ids, affinity, w_gate, w_up, w_down):
+    tok_rows, width = tokens.shape
+    experts = lax.axis_size("expert")
+    sections = lax.axis_size("section")
+    capacity = min(tok_rows, tok_rows * expert_ids.shape[1] * 5 // (4 * experts))
+    core_bit, x_bit, near_bit, far_bit = 1, 2, 4, 8
+
+    def over(flip):
+        return lambda value: lax.ppermute(value, "expert", pairs(experts, flip))
+
+    core, cross_x, near, far = over(core_bit), over(x_bit), over(near_bit), over(far_bit)
+
+    def cross_y(value):
+        return lax.ppermute(value, "section", pairs(sections, 1))
+
+    side = lax.axis_index("section").astype(jnp.int32).reshape(1)
+    table = routing_table(expert_ids, affinity, experts)
+    own, at_x, at_y, at_xy = ([[None, None] for _ in range(4)] for _ in range(4))
+
+    def swap(*slots):
+        for slot in slots:
+            slot[1] = core(slot[0])
+
+    def expert_up(quarter, mine, theirs, ks, *deps):
+        near_rows = [rows for k in ks for rows in mine[k]]
+        far_rows = [rows for k in ks for rows in theirs[k]]
+        near_rows[0] = after(near_rows[0], *deps)
+        return ffn_up(quarter, side, pick, slot_weight, near_rows, far_rows, w_gate[0], w_up[0])
+
+    def expert_down(quarter, hidden_rows, *deps):
+        return ffn_down(quarter, side, put, after(hidden_rows, *deps), w_down[0], width)
+
+    def merge(outs, *deps):
+        swapped = [[core(half[2 * n + 1]) for n in range(2)] for half in outs]
+        return [
+            [joined(after(half[2 * n], *deps), there[n]) for n in range(2)]
+            for half, there in zip(outs, swapped)
+        ]
+
+    def go(hop, value, *deps):
+        return hop(after(value, *deps))
+
+    own[0][0] = restore(tokens, jnp.exp2(exponents.astype(jnp.float32)))
+    own[1][0] = near(own[0][0])
+    at_x[0][0], at_y[0][0] = cross_x(own[0][0]), cross_y(own[0][0])
+    swap(own[0])
+    own[1][0], at_x[0][0], at_y[0][0], table = lax.optimization_barrier(
+        (own[1][0], at_x[0][0], at_y[0][0], table)
+    )
+    own[2][0] = go(far, own[0][0], own[1][0])
+    at_x[1][0], at_y[1][0] = go(cross_x, own[1][0]), go(cross_y, own[1][0])
+    swap(own[1], at_x[0], at_y[0])
+    places = [
+        flip ^ (k * near_bit) ^ plane
+        for ks in ((0, 1), (2, 3))
+        for flip in (0, x_bit)
+        for k in ks
+        for plane in (0, core_bit)
+    ]
+    pick, put, slot_weight = routing_slots(table, places, capacity)
+    at_xy[0][0] = go(cross_x, at_y[0][0], at_x[1][0], put)
+    at_xy[1][0] = go(cross_y, at_x[1][0], at_y[1][0])
+    swap(at_y[1], at_x[1])
+    sum_own, sum_x, sum_y, sum_xy, from_xy = ([None] * 4 for _ in range(5))
+
+    hidden_own = expert_up(0, own, at_y, (0, 1))
+    own[2][0] = after(own[2][0], hidden_own)
+    own[3][0] = go(near, own[2][0])
+    at_x[2][0], at_y[2][0] = go(cross_x, own[2][0]), go(cross_y, own[2][0])
+    swap(own[2], at_xy[0], at_xy[1])
+    hidden_x = expert_up(1, at_x, at_xy, (0, 1))
+    own[3][0] = after(own[3][0], hidden_x)
+    at_x[3][0], at_y[3][0] = go(cross_x, own[3][0]), go(cross_y, own[3][0])
+    swap(own[3], at_x[2], at_y[2])
+    outs_own = expert_down(0, hidden_own, hidden_x)
+    outs_x = expert_down(1, hidden_x, outs_own[1][0])
+    at_xy[2][0] = go(cross_x, at_y[2][0], at_x[3][0])
+    at_xy[3][0] = go(cross_y, at_x[3][0], at_y[3][0])
+    swap(at_x[3], at_y[3])
+    at_xy[2][1], at_xy[3][1] = go(core, at_xy[2][0]), go(core, at_xy[3][0])
+
+    hidden_own = expert_up(2, own, at_y, (2, 3), outs_x[1][0])
+    sum_own[0:2], sum_y[0:2] = merge(outs_own, hidden_own)
+    sum_x[0:2], sum_xy[0:2] = merge(outs_x, hidden_own)
+    from_xy[0] = go(cross_x, sum_xy[0], hidden_own, at_xy[2][0])
+    from_xy[1] = go(cross_y, sum_xy[1], hidden_own, at_xy[3][0])
+    outs_own = expert_down(2, hidden_own)
+
+    hidden_x = expert_up(3, at_x, at_xy, (2, 3), outs_own[1][0])
+    sum_own[2:4], sum_y[2:4] = merge(outs_own, hidden_x)
+    sum_y[0] = joined(sum_y[0], from_xy[0])
+    sum_x[1] = joined(sum_x[1], from_xy[1])
+    from_x1 = go(cross_x, sum_x[1], hidden_x)
+    from_y3 = go(cross_y, sum_y[3], hidden_x)
+    outs = expert_down(3, hidden_x)
+    sum_x[2:4], sum_xy[2:4] = merge(outs)
+
+    from_xy[2] = go(cross_x, sum_xy[2], from_x1)
+    from_xy[3] = go(cross_y, sum_xy[3], from_y3)
+    sum_y[2] = joined(sum_y[2], from_xy[2])
+    sum_x[3] = joined(sum_x[3], from_xy[3])
+    from_y1 = go(cross_y, sum_y[1], from_xy[3])
+    sum_own[3] = joined(sum_own[3], cross_x(sum_x[3]), from_y3)
+    sum_own[1] = joined(sum_own[1], from_x1, from_y1)
+    sum_x[2], sum_y[2], _ = lax.optimization_barrier((sum_x[2], sum_y[2], sum_own[3]))
+    from_near3 = near(sum_own[3])
+    from_x2, from_y2 = cross_x(sum_x[2]), cross_y(sum_y[2])
+    sum_own[2] = joined(sum_own[2], from_x2, from_y2, from_near3)
+    from_far2 = far(sum_own[2])
+    from_near1 = near(after(sum_own[1], from_near3))
+    sum_x[0], sum_y[0], _ = lax.optimization_barrier((sum_x[0], sum_y[0], sum_own[2]))
+    return joined(sum_own[0], cross_x(sum_x[0]), cross_y(sum_y[0]), from_near1, from_far2)
+
+
 def solution(mesh):
+    small = mesh.shape["section"] == 2 and mesh.shape["expert"] == 16
+
+    def body(*operands):
+        return (grid_body if small else exchange_body)(*operands)
+
     return jax.shard_map(
         body,
         mesh=mesh,

time: 988 us -> 458 us (0.46)
  the two profiles are of different devices: /device:TPU:11 before, /device:TPU:0 now
where the time goes in v1:
time: 458 us
  waiting for transfers between devices  256 us (56%)
  Pallas kernels  130 us (28%)
  starting transfers between devices  43.7 us (10%)
  other arithmetic  24.4 us (5%)
    ppermute x50, waiting for transfers between devices, over(): return lambda value: lax.ppermute(value, 'expert', pairs(experts, flip))  158 us
    ppermute x12, waiting for transfers between devices, cross_y(): return lax.ppermute(value, 'section', pairs(sections, 1))  82.1 us
    pallas_call x4, Pallas kernels, ffn_up(): pl.pallas_call(functools.partial(up_kernel, units, cap), out_shape=jax.Sh...  75.6 us
    pallas_call x4, Pallas kernels, ffn_down(): pl.pallas_call(functools.partial(down_kernel, units, cap, half_steps), ou...  51.6 us
    ppermute x50, starting transfers between devices, over(): return lambda value: lax.ppermute(value, 'expert', pairs(experts, flip))  25.2 us
    convert_element_type x16, other arithmetic, joined(): return total.astype(jnp.bfloat16)  19.8 us
    all_to_all x1, waiting for transfers between devices, routing_table(): lax.all_to_all(table, 'expert', split_axis=0, concat_axis=0, tiled=True)  15.8 us
    ppermute x12, starting transfers between devices, cross_y(): return lax.ppermute(value, 'section', pairs(sections, 1))  14.5 us
  transfers between devices with their start and end apart: 63, of which 23 were waited for; matrix products, arithmetic and copies ran while one was open for 5% of the time, Pallas kernels for 28%

profile of v1, /device:TPU:0, one launch (start us, length us, event | category | flops | bytes accessed | tf_op | source)
XLA Modules:
  0.0 457.7 jit_solution(4729306846837817322)
XLA Ops:
  1.5 2.7 restore.1.refs_0_
  4.2 3.1 collective-permute-start
  8.8 1.5 collective-permute-start.2
  11.0 4.0 all-to-all-start
  15.3 15.8 %all-to-all-done = f32[16,1,128]{2,1,0:T(1,128)S(1)} async-done(((f32[16,1,128]{2,1,0:T(1,128)}), f32[16,1,128]{2,1,0:T(1,128)S(1)}, u32[]{:S(2)}, u32[]{:S(2)}) %all-to-all-start) | async-done | bytes 8224 | tf_op jit(solution)/shard_map/all_to_all | solution.py:273
  35.7 17.6 %collective-permute-done.9.refs_2_ = bf16[128,3584]{1,0:T(8,128)(2,1)} collective-permute-done((bf16[128,3584]{1,0:T(8,128)(2,1)S(1)}, bf16[128,3584]{1,0:T(8,128)(2,1)}, u32[]{:S(2)}, u32[]{:S(2)}) %collective-permute-start.9) | collective-permute-done | bytes 917536 | tf_op jit(solution)/shard_map/ppermute | solution.py:300
  53.9 1.5 collective-permute-start.13
  56.5 2.2 collective-permute-start.15
  60.3 14.6 %collective-permute-done.11.refs_4_ = bf16[128,3584]{1,0:T(8,128)(2,1)} collective-permute-done((bf16[128,3584]{1,0:T(8,128)(2,1)}, bf16[128,3584]{1,0:T(8,128)(2,1)}, u32[]{:S(2)}, u32[]{:S(2)}) %collective-permute-start.11) | collective-permute-done | bytes 917536 | tf_op jit(solution)/shard_map/ppermute | solution.py:300
  75.7 18.8 %ffn_up.4.hidden_ref = bf16[320,1024]{1,0:T(8,128)(2,1)} custom-call(s32[1]{0:T(128)} %bitcast.side_ref, bf16[16,80,128]{2,1,0:T(8,128)(2,1)} %fusion.3.pick_ref, f32[1280,1]{1,0:T(8,128)} %reshape.41.weight_ref, bf16[128,3584]{1,0:T(8,128)(2,1)} %restore.1.refs_0_, bf16[128,3584]{1,0:T(8,128)(2,1)} %copy-done.17, bf16[128,3584]{1,0:T(8,128)(2,1)} %copy-done.15, ...), custom_call_target="tpu_custom_call" | custom-call | flops 9395240960 | bytes 36700160 | tf_op jit(solution)/shard_map/ffn_up/pallas_call | solution.py:109
  94.6 5.2 %collective-permute-done.15.refs_0_ = bf16[128,3584]{1,0:T(8,128)(2,1)S(1)} collective-permute-done((bf16[128,3584]{1,0:T(8,128)(2,1)}, bf16[128,3584]{1,0:T(8,128)(2,1)S(1)}, u32[]{:S(2)}, u32[]{:S(2)}) %collective-permute-start.15) | collective-permute-done | bytes 917536 | tf_op jit(solution)/shard_map/ppermute | solution.py:300
  100.4 18.9 %ffn_up.5.hidden_ref = bf16[320,1024]{1,0:T(8,128)(2,1)} custom-call(s32[1]{0:T(128)} %bitcast.side_ref, bf16[16,80,128]{2,1,0:T(8,128)(2,1)} %fusion.3.pick_ref, f32[1280,1]{1,0:T(8,128)} %reshape.41.weight_ref, bf16[128,3584]{1,0:T(8,128)(2,1)} %copy-done.11, bf16[128,3584]{1,0:T(8,128)(2,1)} %collective-permute-done.8.refs_1_, ...), custom_call_target="tpu_custom_call" | custom-call | flops 9395240960 | bytes 36700160 | tf_op jit(solution)/shard_map/ffn_up/pallas_call | solution.py:109
  119.3 2.9 collective-permute-done.17.refs_2_
  124.6 19.2 %collective-permute-done.21.refs_6_ = bf16[128,3584]{1,0:T(8,128)(2,1)} collective-permute-done((bf16[128,3584]{1,0:T(8,128)(2,1)}, bf16[128,3584]{1,0:T(8,128)(2,1)}, u32[]{:S(2)}, u32[]{:S(2)}) %collective-permute-start.21) | collective-permute-done | bytes 917536 | tf_op jit(solution)/shard_map/ppermute | solution.py:305
  143.9 12.9 %ffn_down.4 = (bf16[128,3584]{1,0:T(8,128)(2,1)}, bf16[128,3584]{1,0:T(8,128)(2,1)}, bf16[128,3584]{1,0:T(8,128)(2,1)}, bf16[128,3584]{1,0:T(8,128)(2,1)}, bf16[...) custom-call(s32[1]{0:T(128)} %bitcast.side_ref, ...), custom_call_target="tpu_custom_call" | custom-call | flops 4697620480 | bytes 22020096 | tf_op jit(solution)/shard_map/ffn_down/pallas_call | solution.py:147
  156.8 13.1 %ffn_down.5 = (bf16[128,3584]{1,0:T(8,128)(2,1)}, bf16[128,3584]{1,0:T(8,128)(2,1)}, bf16[128,3584]{1,0:T(8,128)(2,1)}, bf16[128,3584]{1,0:T(8,128)(2,1)}, bf16[...) custom-call(s32[1]{0:T(128)} %bitcast.side_ref, ...), custom_call_target="tpu_custom_call" | custom-call | flops 4697620480 | bytes 22020096 | tf_op jit(solution)/shard_map/ffn_down/pallas_call | solution.py:147
  169.8 1.5 collective-permute-start.30
  172.4 18.8 %ffn_up.6.hidden_ref = bf16[320,1024]{1,0:T(8,128)(2,1)} custom-call(s32[1]{0:T(128)} %bitcast.side_ref, bf16[16,80,128]{2,1,0:T(8,128)(2,1)} %fusion.3.pick_ref, f32[1280,1]{1,0:T(8,128)} %reshape.41.weight_ref, bf16[128,3584]{1,0:T(8,128)(2,1)} %copy-done.12, bf16[128,3584]{1,0:T(8,128)(2,1)} %collective-permute-done.16.refs_1_, ...), custom_call_target="tpu_custom_call" | custom-call | flops 9395240960 | bytes 36700160 | tf_op jit(solution)/shard_map/ffn_up/pallas_call | solution.py:109
  191.2 1.5 collective-permute-done.30.refs_0_
  193.2 2.7 add_convert_fusion.20
  195.9 1.5 collective-permute-start.28
  197.5 2.3 add_convert_fusion.22
  200.3 2.4 add_convert_fusion.13
  202.7 19.2 %collective-permute-done.34.refs_6_ = bf16[128,3584]{1,0:T(8,128)(2,1)} collective-permute-done((bf16[128,3584]{1,0:T(8,128)(2,1)S(1)}, bf16[128,3584]{1,0:T(8,128)(2,1)}, u32[]{:S(2)}, u32[]{:S(2)}) %collective-permute-start.34) | collective-permute-done | bytes 917536 | tf_op jit(solution)/shard_map/ppermute | solution.py:305
  224.1 12.8 %ffn_down.6 = (bf16[128,3584]{1,0:T(8,128)(2,1)}, bf16[128,3584]{1,0:T(8,128)(2,1)}, bf16[128,3584]{1,0:T(8,128)(2,1)}, bf16[128,3584]{1,0:T(8,128)(2,1)}, bf16[...) custom-call(s32[1]{0:T(128)} %bitcast.side_ref, ...), custom_call_target="tpu_custom_call" | custom-call | flops 4697620480 | bytes 22020096 | tf_op jit(solution)/shard_map/ffn_down/pallas_call | solution.py:147
  237.9 19.1 %ffn_up.7.hidden_ref = bf16[320,1024]{1,0:T(8,128)(2,1)} custom-call(s32[1]{0:T(128)} %bitcast.side_ref, bf16[16,80,128]{2,1,0:T(8,128)(2,1)} %fusion.3.pick_ref, f32[1280,1]{1,0:T(8,128)} %reshape.41.weight_ref, bf16[128,3584]{1,0:T(8,128)(2,1)} %collective-permute-done.30.refs_0_, bf16[128,3584]{1,0:T(8,128)(2,1)} %collective-permute-done.31.refs_1_, ...), custom_call_target="tpu_custom_call" | custom-call | flops 9395240960 | bytes 36700160 | tf_op jit(solution)/shard_map/ffn_up/pallas_call | solution.py:109
  257.7 2.6 add_convert_fusion.12
  261.8 12.9 %ffn_down.7 = (bf16[128,3584]{1,0:T(8,128)(2,1)}, bf16[128,3584]{1,0:T(8,128)(2,1)}, bf16[128,3584]{1,0:T(8,128)(2,1)}, bf16[128,3584]{1,0:T(8,128)(2,1)}, bf16[...) custom-call(s32[1]{0:T(128)} %bitcast.side_ref, ...), custom_call_target="tpu_custom_call" | custom-call | flops 4697620480 | bytes 22020096 | tf_op jit(solution)/shard_map/ffn_down/pallas_call | solution.py:147
  274.7 1.5 collective-permute-start.43
  276.2 4.4 collective-permute-done.29
  280.6 1.9 add_convert_fusion.19
  283.7 15.8 %collective-permute-done.43 = bf16[128,3584]{1,0:T(8,128)(2,1)S(1)} collective-permute-done((bf16[128,3584]{1,0:T(8,128)(2,1)}, bf16[128,3584]{1,0:T(8,128)(2,1)S(1)}, u32[]{:S(2)}, u32[]{:S(2)}) %collective-permute-start.43) | collective-permute-done | bytes 917536 | tf_op jit(solution)/shard_map/ppermute | solution.py:300
  299.4 1.6 collective-permute-start.49
  301.3 20.9 %collective-permute-done.49 = bf16[128,3584]{1,0:T(8,128)(2,1)S(1)} collective-permute-done((bf16[128,3584]{1,0:T(8,128)(2,1)S(1)}, bf16[128,3584]{1,0:T(8,128)(2,1)S(1)}, u32[]{:S(2)}, u32[]{:S(2)}) %collective-permute-start.49) | collective-permute-done | bytes 917536 | tf_op jit(solution)/shard_map/ppermute | solution.py:305
  322.2 1.6 collective-permute-start.50
  324.1 20.9 %collective-permute-done.50 = bf16[128,3584]{1,0:T(8,128)(2,1)S(1)} collective-permute-done((bf16[128,3584]{1,0:T(8,128)(2,1)S(1)}, bf16[128,3584]{1,0:T(8,128)(2,1)S(1)}, u32[]{:S(2)}, u32[]{:S(2)}) %collective-permute-start.50) | collective-permute-done | bytes 917536 | tf_op jit(solution)/shard_map/ppermute | solution.py:305
  347.0 20.8 %collective-permute-done.44 = bf16[128,3584]{1,0:T(8,128)(2,1)S(1)} collective-permute-done((bf16[128,3584]{1,0:T(8,128)(2,1)S(1)}, bf16[128,3584]{1,0:T(8,128)(2,1)S(1)}, u32[]{:S(2)}, u32[]{:S(2)}) %collective-permute-start.44) | collective-permute-done | bytes 917536 | tf_op jit(solution)/shard_map/ppermute | solution.py:300
  368.7 1.6 collective-permute-start.59
  370.3 19.3 %collective-permute-done.51 = bf16[128,3584]{1,0:T(8,128)(2,1)S(1)} collective-permute-done((bf16[128,3584]{1,0:T(8,128)(2,1)S(1)}, bf16[128,3584]{1,0:T(8,128)(2,1)S(1)}, u32[]{:S(2)}, u32[]{:S(2)}) %collective-permute-start.51) | collective-permute-done | bytes 917536 | tf_op jit(solution)/shard_map/ppermute | solution.py:300
  391.2 1.5 collective-permute-start.53
  392.8 1.6 add_convert_fusion.1
  394.5 16.9 %collective-permute-done.52 = bf16[128,3584]{1,0:T(8,128)(2,1)S(1)} collective-permute-done((bf16[128,3584]{1,0:T(8,128)(2,1)S(1)}, bf16[128,3584]{1,0:T(8,128)(2,1)S(1)}, u32[]{:S(2)}, u32[]{:S(2)}) %collective-permute-start.52) | collective-permute-done | bytes 917536 | tf_op jit(solution)/shard_map/ppermute | solution.py:300
  412.3 1.5 collective-permute-start.55
  413.8 1.5 collective-permute-start.56
  416.8 15.1 %collective-permute-done.55 = bf16[128,3584]{1,0:T(8,128)(2,1)S(1)} collective-permute-done((bf16[128,3584]{1,0:T(8,128)(2,1)S(1)}, bf16[128,3584]{1,0:T(8,128)(2,1)S(1)}, u32[]{:S(2)}, u32[]{:S(2)}) %collective-permute-start.55) | collective-permute-done | bytes 917536 | tf_op jit(solution)/shard_map/ppermute | solution.py:300
  433.1 18.7 %collective-permute-done.60 = bf16[128,3584]{1,0:T(8,128)(2,1)S(1)} collective-permute-done((bf16[128,3584]{1,0:T(8,128)(2,1)S(1)}, bf16[128,3584]{1,0:T(8,128)(2,1)S(1)}, u32[]{:S(2)}, u32[]{:S(2)}) %collective-permute-start.60) | collective-permute-done | bytes 917536 | tf_op jit(solution)/shard_map/ppermute | solution.py:300
  451.8 4.3 collective-permute-done.61
  456.1 1.6 add_convert_fusion
  (186 shorter events, 32.9 us)
Async XLA Ops:
  4.2 26.9 %collective-permute-start = (bf16[128,3584]{1,0:T(8,128)(2,1)}, bf16[128,3584]{1,0:T(8,128)(2,1)S(1)}, u32[]{:S(2)}, u32[]{:S(2)}) collective-permute-start(bf16[128,3584]{1,0:T(8,128)(2,1)} %restore.1.refs_0_), channel_id=1, source_target_pairs={{0,4},{1,5},{2,6},{3,7},{4,0},{5,1},{6,2},{7,3},{8,12},{9,13},{10,... | collective-permute-start | bytes 2752520 | tf_op jit(solution)/shard_map/ppermute | solution.py:300
  7.3 23.8 %collective-permute-start.1 = (bf16[128,3584]{1,0:T(8,128)(2,1)}, bf16[128,3584]{1,0:T(8,128)(2,1)S(1)}, u32[]{:S(2)}, u32[]{:S(2)}) collective-permute-start(bf16[128,3584]{1,0:T(8,128)(2,1)} %restore.1.refs_0_), channel_id=1, source_target_pairs={{0,2},{1,3},{2,0},{3,1},{4,6},{5,7},{6,4},{7,5},{8,10},{9,11},{10,... | collective-permute-start | bytes 2752520 | tf_op jit(solution)/shard_map/ppermute | solution.py:300
  8.8 22.3 %collective-permute-start.2 = (bf16[128,3584]{1,0:T(8,128)(2,1)}, bf16[128,3584]{1,0:T(8,128)(2,1)}, u32[]{:S(2)}, u32[]{:S(2)}) collective-permute-start(bf16[128,3584]{1,0:T(8,128)(2,1)} %restore.1.refs_0_), channel_id=1, source_target_pairs={{0,16},{16,0},{1,17},{17,1},{2,18},{18,2},{3,19},{19,3},{4,20},{20... | collective-permute-start | bytes 2752520 | tf_op jit(solution)/shard_map/ppermute | solution.py:305
  14.9 40.5 %collective-permute-start.3 = (bf16[128,3584]{1,0:T(8,128)(2,1)}, bf16[128,3584]{1,0:T(8,128)(2,1)S(1)}, u32[]{:S(2)}, u32[]{:S(2)}) collective-permute-start(bf16[128,3584]{1,0:T(8,128)(2,1)} %restore.1.refs_0_), channel_id=1, source_target_pairs={{0,1},{1,0},{2,3},{3,2},{4,5},{5,4},{6,7},{7,6},{8,9},{9,8},{10,11... | collective-permute-start | bytes 2752520 | tf_op jit(solution)/shard_map/ppermute | solution.py:300
  31.1 22.2 %collective-permute-start.9 = (bf16[128,3584]{1,0:T(8,128)(2,1)S(1)}, bf16[128,3584]{1,0:T(8,128)(2,1)}, u32[]{:S(2)}, u32[]{:S(2)}) collective-permute-start(bf16[128,3584]{1,0:T(8,128)(2,1)S(1)} %collective-permute-done.refs_2_), channel_id=1, source_target_pairs={{0,2},{1,3},{2,0},{3,1},{4,6},{5,7},{6,4},{7,5},{8,10},{9,11},{10,... | collective-permute-start | bytes 2752520 | tf_op jit(solution)/shard_map/ppermute | solution.py:300
  31.7 22.2 %collective-permute-start.6 = (bf16[128,3584]{1,0:T(8,128)(2,1)S(1)}, bf16[128,3584]{1,0:T(8,128)(2,1)}, u32[]{:S(2)}, u32[]{:S(2)}) collective-permute-start(bf16[128,3584]{1,0:T(8,128)(2,1)S(1)} %collective-permute-done.refs_2_), channel_id=1, source_target_pairs={{0,16},{16,0},{1,17},{17,1},{2,18},{18,2},{3,19},{19,3},{4,20},{20... | collective-permute-start | bytes 2752520 | tf_op jit(solution)/shard_map/ppermute | solution.py:305
  33.3 23.3 %collective-permute-start.4 = (bf16[128,3584]{1,0:T(8,128)(2,1)S(1)}, bf16[128,3584]{1,0:T(8,128)(2,1)}, u32[]{:S(2)}, u32[]{:S(2)}) collective-permute-start(bf16[128,3584]{1,0:T(8,128)(2,1)S(1)} %collective-permute-done.refs_2_), channel_id=1, source_target_pairs={{0,1},{1,0},{2,3},{3,2},{4,5},{5,4},{6,7},{7,6},{8,9},{9,8},{10,11... | collective-permute-start | bytes 2752520 | tf_op jit(solution)/shard_map/ppermute | solution.py:300
  33.3 26.9 %collective-permute-start.5 = (bf16[128,3584]{1,0:T(8,128)(2,1)}, bf16[128,3584]{1,0:T(8,128)(2,1)}, u32[]{:S(2)}, u32[]{:S(2)}) collective-permute-start(bf16[128,3584]{1,0:T(8,128)(2,1)} %collective-permute-done.2.refs_4_), channel_id=1, source_target_pairs={{0,1},{1,0},{2,3},{3,2},{4,5},{5,4},{6,7},{7,6},{8,9},{9,8},{10,11... | collective-permute-start | bytes 2752520 | tf_op jit(solution)/shard_map/ppermute | solution.py:300
  56.5 43.3 %collective-permute-start.15 = (bf16[128,3584]{1,0:T(8,128)(2,1)}, bf16[128,3584]{1,0:T(8,128)(2,1)S(1)}, u32[]{:S(2)}, u32[]{:S(2)}) collective-permute-start(bf16[128,3584]{1,0:T(8,128)(2,1)} %restore.1.refs_0_), channel_id=1, source_target_pairs={{0,8},{1,9},{2,10},{3,11},{4,12},{5,13},{6,14},{7,15},{8,0},{9,1},... | collective-permute-start | bytes 2752520 | tf_op jit(solution)/shard_map/ppermute | solution.py:300
  60.3 39.5 %collective-permute-start.8 = (bf16[128,3584]{1,0:T(8,128)(2,1)S(1)}, bf16[128,3584]{1,0:T(8,128)(2,1)}, u32[]{:S(2)}, u32[]{:S(2)}) collective-permute-start(bf16[128,3584]{1,0:T(8,128)(2,1)S(1)} %collective-permute-done.1.refs_0_), channel_id=1, source_target_pairs={{0,1},{1,0},{2,3},{3,2},{4,5},{5,4},{6,7},{7,6},{8,9},{9,8},{10,11... | collective-permute-start | bytes 2752520 | tf_op jit(solution)/shard_map/ppermute | solution.py:300
  74.9 25.5 %collective-permute-start.10 = (bf16[128,3584]{1,0:T(8,128)(2,1)}, bf16[128,3584]{1,0:T(8,128)(2,1)}, u32[]{:S(2)}, u32[]{:S(2)}) collective-permute-start(bf16[128,3584]{1,0:T(8,128)(2,1)} %collective-permute-done.9.refs_2_), channel_id=1, source_target_pairs={{0,1},{1,0},{2,3},{3,2},{4,5},{5,4},{6,7},{7,6},{8,9},{9,8},{10,11... | collective-permute-start | bytes 2752520 | tf_op jit(solution)/shard_map/ppermute | solution.py:300
  75.2 25.2 %collective-permute-start.12 = (bf16[128,3584]{1,0:T(8,128)(2,1)}, bf16[128,3584]{1,0:T(8,128)(2,1)}, u32[]{:S(2)}, u32[]{:S(2)}) collective-permute-start(bf16[128,3584]{1,0:T(8,128)(2,1)} %collective-permute-done.11.refs_4_), channel_id=1, source_target_pairs={{0,1},{1,0},{2,3},{3,2},{4,5},{5,4},{6,7},{7,6},{8,9},{9,8},{10,11... | collective-permute-start | bytes 2752520 | tf_op jit(solution)/shard_map/ppermute | solution.py:300
  75.4 25.0 %collective-permute-start.14 = (bf16[128,3584]{1,0:T(8,128)(2,1)}, bf16[128,3584]{1,0:T(8,128)(2,1)}, u32[]{:S(2)}, u32[]{:S(2)}) collective-permute-start(bf16[128,3584]{1,0:T(8,128)(2,1)} %collective-permute-done.13.refs_6_), channel_id=1, source_target_pairs={{0,1},{1,0},{2,3},{3,2},{4,5},{5,4},{6,7},{7,6},{8,9},{9,8},{10,11... | collective-permute-start | bytes 2752520 | tf_op jit(solution)/shard_map/ppermute | solution.py:300
  99.8 22.4 %collective-permute-start.17 = (bf16[128,3584]{1,0:T(8,128)(2,1)S(1)}, bf16[128,3584]{1,0:T(8,128)(2,1)}, u32[]{:S(2)}, u32[]{:S(2)}) collective-permute-start(bf16[128,3584]{1,0:T(8,128)(2,1)S(1)} %collective-permute-done.15.refs_0_), channel_id=1, source_target_pairs={{0,4},{1,5},{2,6},{3,7},{4,0},{5,1},{6,2},{7,3},{8,12},{9,13},{10,... | collective-permute-start | bytes 2752520 | tf_op jit(solution)/shard_map/ppermute | solution.py:300
  99.8 24.6 %collective-permute-start.19 = (bf16[128,3584]{1,0:T(8,128)(2,1)S(1)}, bf16[128,3584]{1,0:T(8,128)(2,1)S(1)}, u32[]{:S(2)}, u32[]{:S(2)}) collective-permute-start(bf16[128,3584]{1,0:T(8,128)(2,1)S(1)} %collective-permute-done.15.refs_0_), channel_id=1, source_target_pairs={{0,16},{16,0},{1,17},{17,1},{2,18},{18,2},{3,19},{19,3},{4,20},{20... | collective-permute-start | bytes 2752520 | tf_op jit(solution)/shard_map/ppermute | solution.py:305
  122.2 21.7 %collective-permute-start.21 = (bf16[128,3584]{1,0:T(8,128)(2,1)}, bf16[128,3584]{1,0:T(8,128)(2,1)}, u32[]{:S(2)}, u32[]{:S(2)}) collective-permute-start(bf16[128,3584]{1,0:T(8,128)(2,1)} %collective-permute-done.17.refs_2_), channel_id=1, source_target_pairs={{0,16},{16,0},{1,17},{17,1},{2,18},{18,2},{3,19},{19,3},{4,20},{20... | collective-permute-start | bytes 2752520 | tf_op jit(solution)/shard_map/ppermute | solution.py:305
  122.7 47.1 %collective-permute-start.16 = (bf16[128,3584]{1,0:T(8,128)(2,1)S(1)}, bf16[128,3584]{1,0:T(8,128)(2,1)}, u32[]{:S(2)}, u32[]{:S(2)}) collective-permute-start(bf16[128,3584]{1,0:T(8,128)(2,1)S(1)} %collective-permute-done.15.refs_0_), channel_id=1, source_target_pairs={{0,1},{1,0},{2,3},{3,2},{4,5},{5,4},{6,7},{7,6},{8,9},{9,8},{10,11... | collective-permute-start | bytes 2752520 | tf_op jit(solution)/shard_map/ppermute | solution.py:300
  122.7 48.7 %collective-permute-start.27 = (bf16[128,3584]{1,0:T(8,128)(2,1)}, bf16[128,3584]{1,0:T(8,128)(2,1)S(1)}, u32[]{:S(2)}, u32[]{:S(2)}) collective-permute-start(bf16[128,3584]{1,0:T(8,128)(2,1)} %collective-permute-done.17.refs_2_), channel_id=1, source_target_pairs={{0,2},{1,3},{2,0},{3,1},{4,6},{5,7},{6,4},{7,5},{8,10},{9,11},{10,... | collective-permute-start | bytes 2752520 | tf_op jit(solution)/shard_map/ppermute | solution.py:300
  124.1 47.4 %collective-permute-start.18 = (bf16[128,3584]{1,0:T(8,128)(2,1)}, bf16[128,3584]{1,0:T(8,128)(2,1)}, u32[]{:S(2)}, u32[]{:S(2)}) collective-permute-start(bf16[128,3584]{1,0:T(8,128)(2,1)} %collective-permute-done.17.refs_2_), channel_id=1, source_target_pairs={{0,1},{1,0},{2,3},{3,2},{4,5},{5,4},{6,7},{7,6},{8,9},{9,8},{10,11... | collective-permute-start | bytes 2752520 | tf_op jit(solution)/shard_map/ppermute | solution.py:300
  124.4 47.5 %collective-permute-start.20 = (bf16[128,3584]{1,0:T(8,128)(2,1)S(1)}, bf16[128,3584]{1,0:T(8,128)(2,1)}, u32[]{:S(2)}, u32[]{:S(2)}) collective-permute-start(bf16[128,3584]{1,0:T(8,128)(2,1)S(1)} %collective-permute-done.19.refs_4_), channel_id=1, source_target_pairs={{0,1},{1,0},{2,3},{3,2},{4,5},{5,4},{6,7},{7,6},{8,9},{9,8},{10,11... | collective-permute-start | bytes 2752520 | tf_op jit(solution)/shard_map/ppermute | solution.py:300
  143.9 28.2 %collective-permute-start.22 = (bf16[128,3584]{1,0:T(8,128)(2,1)}, bf16[128,3584]{1,0:T(8,128)(2,1)}, u32[]{:S(2)}, u32[]{:S(2)}) collective-permute-start(bf16[128,3584]{1,0:T(8,128)(2,1)} %collective-permute-done.21.refs_6_), channel_id=1, source_target_pairs={{0,1},{1,0},{2,3},{3,2},{4,5},{5,4},{6,7},{7,6},{8,9},{9,8},{10,11... | collective-permute-start | bytes 2752520 | tf_op jit(solution)/shard_map/ppermute | solution.py:300
  169.8 22.9 %collective-permute-start.30 = (bf16[128,3584]{1,0:T(8,128)(2,1)S(1)}, bf16[128,3584]{1,0:T(8,128)(2,1)}, u32[]{:S(2)}, u32[]{:S(2)}) collective-permute-start(bf16[128,3584]{1,0:T(8,128)(2,1)S(1)} %collective-permute-done.15.refs_0_), channel_id=1, source_target_pairs={{0,2},{1,3},{2,0},{3,1},{4,6},{5,7},{6,4},{7,5},{8,10},{9,11},{10,... | collective-permute-start | bytes 2752520 | tf_op jit(solution)/shard_map/ppermute | solution.py:300
  171.6 24.4 %collective-permute-start.24 = (bf16[128,3584]{1,0:T(8,128)(2,1)}, bf16[128,3584]{1,0:T(8,128)(2,1)}, u32[]{:S(2)}, u32[]{:S(2)}) collective-permute-start(bf16[128,3584]{1,0:T(8,128)(2,1)} %get-tuple-element.95), channel_id=1, source_target_pairs={{0,1},{1,0},{2,3},{3,2},{4,5},{5,4},{6,7},{7,6},{8,9},{9,8},{10,11... | collective-permute-start | bytes 2752520 | tf_op jit(solution)/shard_map/ppermute | solution.py:300
  171.9 27.9 %collective-permute-start.41 = (bf16[128,3584]{1,0:T(8,128)(2,1)}, bf16[128,3584]{1,0:T(8,128)(2,1)}, u32[]{:S(2)}, u32[]{:S(2)}) collective-permute-start(bf16[128,3584]{1,0:T(8,128)(2,1)} %get-tuple-element.119), channel_id=1, source_target_pairs={{0,1},{1,0},{2,3},{3,2},{4,5},{5,4},{6,7},{7,6},{8,9},{9,8},{10,11... | collective-permute-start | bytes 2752520 | tf_op jit(solution)/shard_map/ppermute | solution.py:300
  172.1 84.9 %collective-permute-start.40 = (bf16[128,3584]{1,0:T(8,128)(2,1)}, bf16[128,3584]{1,0:T(8,128)(2,1)S(1)}, u32[]{:S(2)}, u32[]{:S(2)}) collective-permute-start(bf16[128,3584]{1,0:T(8,128)(2,1)} %get-tuple-element.116), channel_id=1, source_target_pairs={{0,1},{1,0},{2,3},{3,2},{4,5},{5,4},{6,7},{7,6},{8,9},{9,8},{10,11... | collective-permute-start | bytes 2752520 | tf_op jit(solution)/shard_map/ppermute | solution.py:300
  192.7 30.9 %collective-permute-start.31 = (bf16[128,3584]{1,0:T(8,128)(2,1)}, bf16[128,3584]{1,0:T(8,128)(2,1)}, u32[]{:S(2)}, u32[]{:S(2)}) collective-permute-start(bf16[128,3584]{1,0:T(8,128)(2,1)} %collective-permute-done.30.refs_0_), channel_id=1, source_target_pairs={{0,1},{1,0},{2,3},{3,2},{4,5},{5,4},{6,7},{7,6},{8,9},{9,8},{10,11... | collective-permute-start | bytes 2752520 | tf_op jit(solution)/shard_map/ppermute | solution.py:300
  195.9 25.9 %collective-permute-start.28 = (bf16[128,3584]{1,0:T(8,128)(2,1)S(1)}, bf16[128,3584]{1,0:T(8,128)(2,1)}, u32[]{:S(2)}, u32[]{:S(2)}) collective-permute-start(bf16[128,3584]{1,0:T(8,128)(2,1)S(1)} %copy-done.14), channel_id=1, source_target_pairs={{0,2},{1,3},{2,0},{3,1},{4,6},{5,7},{6,4},{7,5},{8,10},{9,11},{10,... | collective-permute-start | bytes 2752520 | tf_op jit(solution)/shard_map/ppermute | solution.py:300
  199.8 22.1 %collective-permute-start.34 = (bf16[128,3584]{1,0:T(8,128)(2,1)S(1)}, bf16[128,3584]{1,0:T(8,128)(2,1)}, u32[]{:S(2)}, u32[]{:S(2)}) collective-permute-start(bf16[128,3584]{1,0:T(8,128)(2,1)S(1)} %collective-permute-done.27.refs_2_), channel_id=1, source_target_pairs={{0,16},{16,0},{1,17},{17,1},{2,18},{18,2},{3,19},{19,3},{4,20},{20... | collective-permute-start | bytes 2752520 | tf_op jit(solution)/shard_map/ppermute | solution.py:305
  202.7 34.3 %collective-permute-start.32 = (bf16[128,3584]{1,0:T(8,128)(2,1)S(1)}, bf16[128,3584]{1,0:T(8,128)(2,1)S(1)}, u32[]{:S(2)}, u32[]{:S(2)}) collective-permute-start(bf16[128,3584]{1,0:T(8,128)(2,1)S(1)} %collective-permute-done.27.refs_2_), channel_id=1, source_target_pairs={{0,1},{1,0},{2,3},{3,2},{4,5},{5,4},{6,7},{7,6},{8,9},{9,8},{10,11... | collective-permute-start | bytes 2752520 | tf_op jit(solution)/shard_map/ppermute | solution.py:300
  223.6 34.0 %collective-permute-start.42 = (bf16[128,3584]{1,0:T(8,128)(2,1)}, bf16[128,3584]{1,0:T(8,128)(2,1)}, u32[]{:S(2)}, u32[]{:S(2)}) collective-permute-start(bf16[128,3584]{1,0:T(8,128)(2,1)} %add_convert_fusion.13), channel_id=1, source_target_pairs={{0,16},{16,0},{1,17},{17,1},{2,18},{18,2},{3,19},{19,3},{4,20},{20... | collective-permute-start | bytes 2752520 | tf_op jit(solution)/shard_map/ppermute | solution.py:305
  237.0 37.7 %collective-permute-start.25 = (bf16[128,3584]{1,0:T(8,128)(2,1)}, bf16[128,3584]{1,0:T(8,128)(2,1)}, u32[]{:S(2)}, u32[]{:S(2)}) collective-permute-start(bf16[128,3584]{1,0:T(8,128)(2,1)} %get-tuple-element.97), channel_id=1, source_target_pairs={{0,1},{1,0},{2,3},{3,2},{4,5},{5,4},{6,7},{7,6},{8,9},{9,8},{10,11... | collective-permute-start | bytes 2752520 | tf_op jit(solution)/shard_map/ppermute | solution.py:300
  237.1 153.6 %collective-permute-start.57 = (bf16[128,3584]{1,0:T(8,128)(2,1)}, bf16[128,3584]{1,0:T(8,128)(2,1)}, u32[]{:S(2)}, u32[]{:S(2)}) collective-permute-start(bf16[128,3584]{1,0:T(8,128)(2,1)} %get-tuple-element.141), channel_id=1, source_target_pairs={{0,1},{1,0},{2,3},{3,2},{4,5},{5,4},{6,7},{7,6},{8,9},{9,8},{10,11... | collective-permute-start | bytes 2752520 | tf_op jit(solution)/shard_map/ppermute | solution.py:300
  237.9 178.9 %collective-permute-start.23 = (bf16[128,3584]{1,0:T(8,128)(2,1)}, bf16[128,3584]{1,0:T(8,128)(2,1)S(1)}, u32[]{:S(2)}, u32[]{:S(2)}) collective-permute-start(bf16[128,3584]{1,0:T(8,128)(2,1)} %get-tuple-element.92), channel_id=1, source_target_pairs={{0,1},{1,0},{2,3},{3,2},{4,5},{5,4},{6,7},{7,6},{8,9},{9,8},{10,11... | collective-permute-start | bytes 2752520 | tf_op jit(solution)/shard_map/ppermute | solution.py:300
  257.0 23.6 %collective-permute-start.29 = (bf16[128,3584]{1,0:T(8,128)(2,1)}, bf16[128,3584]{1,0:T(8,128)(2,1)}, u32[]{:S(2)}, u32[]{:S(2)}) collective-permute-start(bf16[128,3584]{1,0:T(8,128)(2,1)} %add_convert_fusion.20), channel_id=1, source_target_pairs={{0,2},{1,3},{2,0},{3,1},{4,6},{5,7},{6,4},{7,5},{8,10},{9,11},{10,... | collective-permute-start | bytes 2752520 | tf_op jit(solution)/shard_map/ppermute | solution.py:300
  260.3 85.6 %collective-permute-start.38 = (bf16[128,3584]{1,0:T(8,128)(2,1)}, bf16[128,3584]{1,0:T(8,128)(2,1)S(1)}, u32[]{:S(2)}, u32[]{:S(2)}) collective-permute-start(bf16[128,3584]{1,0:T(8,128)(2,1)} %get-tuple-element.111), channel_id=1, source_target_pairs={{0,1},{1,0},{2,3},{3,2},{4,5},{5,4},{6,7},{7,6},{8,9},{9,8},{10,11... | collective-permute-start | bytes 2752520 | tf_op jit(solution)/shard_map/ppermute | solution.py:300
  274.7 24.7 %collective-permute-start.43 = (bf16[128,3584]{1,0:T(8,128)(2,1)}, bf16[128,3584]{1,0:T(8,128)(2,1)S(1)}, u32[]{:S(2)}, u32[]{:S(2)}) collective-permute-start(bf16[128,3584]{1,0:T(8,128)(2,1)} %add_convert_fusion.12), channel_id=1, source_target_pairs={{0,2},{1,3},{2,0},{3,1},{4,6},{5,7},{6,4},{7,5},{8,10},{9,11},{10,... | collective-permute-start | bytes 2752520 | tf_op jit(solution)/shard_map/ppermute | solution.py:300
  299.4 22.8 %collective-permute-start.37 = (bf16[128,3584]{1,0:T(8,128)(2,1)S(1)}, bf16[128,3584]{1,0:T(8,128)(2,1)S(1)}, u32[]{:S(2)}, u32[]{:S(2)}) collective-permute-start(bf16[128,3584]{1,0:T(8,128)(2,1)S(1)} %copy-done.32), channel_id=1, source_target_pairs={{0,1},{1,0},{2,3},{3,2},{4,5},{5,4},{6,7},{7,6},{8,9},{9,8},{10,11... | collective-permute-start | bytes 2752520 | tf_op jit(solution)/shard_map/ppermute | solution.py:300
  299.4 22.8 %collective-permute-start.49 = (bf16[128,3584]{1,0:T(8,128)(2,1)S(1)}, bf16[128,3584]{1,0:T(8,128)(2,1)S(1)}, u32[]{:S(2)}, u32[]{:S(2)}) collective-permute-start(bf16[128,3584]{1,0:T(8,128)(2,1)S(1)} %copy-done.23), channel_id=1, source_target_pairs={{0,16},{16,0},{1,17},{17,1},{2,18},{18,2},{3,19},{19,3},{4,20},{20... | collective-permute-start | bytes 2752520 | tf_op jit(solution)/shard_map/ppermute | solution.py:305
  322.2 22.8 %collective-permute-start.46 = (bf16[128,3584]{1,0:T(8,128)(2,1)S(1)}, bf16[128,3584]{1,0:T(8,128)(2,1)S(1)}, u32[]{:S(2)}, u32[]{:S(2)}) collective-permute-start(bf16[128,3584]{1,0:T(8,128)(2,1)S(1)} %copy-done.31), channel_id=1, source_target_pairs={{0,1},{1,0},{2,3},{3,2},{4,5},{5,4},{6,7},{7,6},{8,9},{9,8},{10,11... | collective-permute-start | bytes 2752520 | tf_op jit(solution)/shard_map/ppermute | solution.py:300
  322.2 22.8 %collective-permute-start.50 = (bf16[128,3584]{1,0:T(8,128)(2,1)S(1)}, bf16[128,3584]{1,0:T(8,128)(2,1)S(1)}, u32[]{:S(2)}, u32[]{:S(2)}) collective-permute-start(bf16[128,3584]{1,0:T(8,128)(2,1)S(1)} %add_convert_fusion.8), channel_id=1, source_target_pairs={{0,16},{16,0},{1,17},{17,1},{2,18},{18,2},{3,19},{19,3},{4,20},{20... | collective-permute-start | bytes 2752520 | tf_op jit(solution)/shard_map/ppermute | solution.py:305
  345.0 23.7 %collective-permute-start.45 = (bf16[128,3584]{1,0:T(8,128)(2,1)S(1)}, bf16[128,3584]{1,0:T(8,128)(2,1)S(1)}, u32[]{:S(2)}, u32[]{:S(2)}) collective-permute-start(bf16[128,3584]{1,0:T(8,128)(2,1)S(1)} %copy-done.30), channel_id=1, source_target_pairs={{0,1},{1,0},{2,3},{3,2},{4,5},{5,4},{6,7},{7,6},{8,9},{9,8},{10,11... | collective-permute-start | bytes 2752520 | tf_op jit(solution)/shard_map/ppermute | solution.py:300
  345.0 22.8 %collective-permute-start.44 = (bf16[128,3584]{1,0:T(8,128)(2,1)S(1)}, bf16[128,3584]{1,0:T(8,128)(2,1)S(1)}, u32[]{:S(2)}, u32[]{:S(2)}) collective-permute-start(bf16[128,3584]{1,0:T(8,128)(2,1)S(1)} %add_convert_fusion.15), channel_id=1, source_target_pairs={{0,2},{1,3},{2,0},{3,1},{4,6},{5,7},{6,4},{7,5},{8,10},{9,11},{10,... | collective-permute-start | bytes 2752520 | tf_op jit(solution)/shard_map/ppermute | solution.py:300
  346.8 47.7 %collective-permute-start.36 = (bf16[128,3584]{1,0:T(8,128)(2,1)S(1)}, bf16[128,3584]{1,0:T(8,128)(2,1)S(1)}, u32[]{:S(2)}, u32[]{:S(2)}) collective-permute-start(bf16[128,3584]{1,0:T(8,128)(2,1)S(1)} %copy-done.29), channel_id=1, source_target_pairs={{0,1},{1,0},{2,3},{3,2},{4,5},{5,4},{6,7},{7,6},{8,9},{9,8},{10,11... | collective-permute-start | bytes 2752520 | tf_op jit(solution)/shard_map/ppermute | solution.py:300
  367.7 21.8 %collective-permute-start.51 = (bf16[128,3584]{1,0:T(8,128)(2,1)S(1)}, bf16[128,3584]{1,0:T(8,128)(2,1)S(1)}, u32[]{:S(2)}, u32[]{:S(2)}) collective-permute-start(bf16[128,3584]{1,0:T(8,128)(2,1)S(1)} %add_convert_fusion.6), channel_id=1, source_target_pairs={{0,2},{1,3},{2,0},{3,1},{4,6},{5,7},{6,4},{7,5},{8,10},{9,11},{10,... | collective-permute-start | bytes 2752520 | tf_op jit(solution)/shard_map/ppermute | solution.py:300
  368.7 22.6 %collective-permute-start.59 = (bf16[128,3584]{1,0:T(8,128)(2,1)S(1)}, bf16[128,3584]{1,0:T(8,128)(2,1)S(1)}, u32[]{:S(2)}, u32[]{:S(2)}) collective-permute-start(bf16[128,3584]{1,0:T(8,128)(2,1)S(1)} %copy-done.8), channel_id=1, source_target_pairs={{0,16},{16,0},{1,17},{17,1},{2,18},{18,2},{3,19},{19,3},{4,20},{20... | collective-permute-start | bytes 2752520 | tf_op jit(solution)/shard_map/ppermute | solution.py:305
  390.0 21.6 %collective-permute-start.54 = (bf16[128,3584]{1,0:T(8,128)(2,1)S(1)}, bf16[128,3584]{1,0:T(8,128)(2,1)S(1)}, u32[]{:S(2)}, u32[]{:S(2)}) collective-permute-start(bf16[128,3584]{1,0:T(8,128)(2,1)S(1)} %add_convert_fusion.5), channel_id=1, source_target_pairs={{0,4},{1,5},{2,6},{3,7},{4,0},{5,1},{6,2},{7,3},{8,12},{9,13},{10,... | collective-permute-start | bytes 2752520 | tf_op jit(solution)/shard_map/ppermute | solution.py:300
  415.3 36.5 %collective-permute-start.60 = (bf16[128,3584]{1,0:T(8,128)(2,1)S(1)}, bf16[128,3584]{1,0:T(8,128)(2,1)S(1)}, u32[]{:S(2)}, u32[]{:S(2)}) collective-permute-start(bf16[128,3584]{1,0:T(8,128)(2,1)S(1)} %add_convert_fusion.1), channel_id=1, source_target_pairs={{0,4},{1,5},{2,6},{3,7},{4,0},{5,1},{6,2},{7,3},{8,12},{9,13},{10,... | collective-permute-start | bytes 2752520 | tf_op jit(solution)/shard_map/ppermute | solution.py:300
  416.8 39.3 %collective-permute-start.61 = (bf16[128,3584]{1,0:T(8,128)(2,1)S(1)}, bf16[128,3584]{1,0:T(8,128)(2,1)S(1)}, u32[]{:S(2)}, u32[]{:S(2)}) collective-permute-start(bf16[128,3584]{1,0:T(8,128)(2,1)S(1)} %add_convert_fusion.4), channel_id=1, source_target_pairs={{0,8},{1,9},{2,10},{3,11},{4,12},{5,13},{6,14},{7,15},{8,0},{9,1},... | collective-permute-start | bytes 2752520 | tf_op jit(solution)/shard_map/ppermute | solution.py:300
  (49 other events, 1062.2 us)
